TPU v7x, 256 devices: a whole 4x4x8 slice. The times are simulated.
256 devices in a mesh: ax: 64 (over y_lo, z, x), sec: 4 (over y_hi, core).
Axes of the slice: x: 4, y: 4 (y_hi: 2, y_lo: 2; y = y_hi * 2 + y_lo), z: 8, core: 2. Of those that a mesh axis runs over, the one named last changes fastest.
Arguments:
- load: float32 [8192, 6, 1024], P('ax', None, 'sec'), may hold values from -6 to 6
- disp: float32 [8192, 6, 1024], P('ax', None, 'sec'), may hold values from -1.5 to 1.5
- stiff: float32 [8192, 6, 1024], P('ax', None, 'sec'), may hold values from 0.5 to 2
- hole: int32 [8192, 1024], P('ax', 'sec'), may hold values 0 or 1
- section_class: int32 [8192], P('ax'), may hold values from 0 to 3
- class_table: float32 [4, 6], replicated, may hold values from 0.5 to 2
- precond: float32 [6, 6, 1024], replicated, may hold values from -0.5 to 0.5, as said below
Outputs:
- disp_new: float32 [8192, 6, 1024], P('ax', None, 'sec')
- residual_new: float32 [8192, 6, 1024], P('ax', None, 'sec')
- stats: float32 [3], replicated
Inputs may be any that keep to these rules, and one draw needn't show every extreme that they name: `precond`: for each harmonic the matrix over the first two dimensions is symmetric and positive definite.
All inputs are finite; a program needn't handle non-finite values. No bound on the sum of `hole` on one device may be relied on, other than what follows from the above.
Results may differ from a plain program's by a relative error of at most 0.0075.
Values sent between devices are 32-bit elements; how exact they have to be, the bound alone decides.
A program may use at most 64 MiB of HBM per device.

v0:
```python
import math
import jax
import jax.numpy as jnp
from jax import lax
from jax.sharding import PartitionSpec as P


def with_halo(x, sides, width, wrap):
    for axis, dim in sides:
        size, length = (lax.axis_size(axis), x.shape[dim])
        up = [(i, (i + 1) % size) for i in range(size if wrap else size - 1)]
        down = [(j, i) for i, j in up]
        last = lax.slice_in_dim(x, length - width, length, axis=dim)
        first = lax.slice_in_dim(x, 0, width, axis=dim)
        before = lax.ppermute(last, axis, up)
        after = lax.ppermute(first, axis, down)
        x = jnp.concatenate([before, x, after], axis=dim)
    return x


def swap_radial(field):
    extent = field.shape
    folded = field.reshape(extent[0], extent[1] // 2, 2, extent[2])
    return jnp.flip(folded, axis=2).reshape(extent)


def apply_operator(field, stiffness):
    axial_pad = with_halo(field, (("ax", 0),), 1, False)
    sector_pad = with_halo(field, (("sec", 2),), 1, True)
    beside = axial_pad[2:] + axial_pad[:-2]
    beside = beside + sector_pad[:, :, 2:] + sector_pad[:, :, :-2]
    return (stiffness + 4.5) * field - beside - 0.5 * swap_radial(field)


def harmonic_table(row_index, col_index, length):
    product = row_index[:, None] * col_index[None, :] % length
    angle = 2.0 * math.pi / length * product.astype(jnp.float32)
    return jnp.concatenate([jnp.cos(angle), jnp.sin(angle)], axis=1)


def scale_harmonics(block_inverse, spectrum):
    doubled = jnp.concatenate([block_inverse, block_inverse], axis=2)
    return jnp.sum(doubled[None] * spectrum[:, None], axis=2)


def shards(load, disp, stiff, hole, section_class, class_table, precond):
    slab_count, comp_count, sector_width = disp.shape
    sector_count = lax.axis_size("sec")
    around_cells = sector_width * sector_count
    total_axial = slab_count * lax.axis_size("ax")
    position = lax.axis_index("ax") * slab_count + jnp.arange(slab_count)
    taper = 1.0 + 2.0 * position.astype(jnp.float32) / (total_axial - 1)
    one_hot = (section_class[:, None] == jnp.arange(class_table.shape[0])[None, :]).astype(
        jnp.float32
    )
    factors = jnp.dot(one_hot, class_table, precision=lax.Precision.HIGHEST)
    stiffness = stiff * (factors * taper[:, None])[:, :, None]
    solid = (1 - hole).astype(jnp.float32)[:, None, :]
    residual = solid * (load - apply_operator(disp, stiffness))
    sector = lax.axis_index("sec")
    own_index = sector * sector_width + jnp.arange(sector_width)
    table = harmonic_table(jnp.arange(around_cells), own_index, around_cells)
    own_inverse = lax.dynamic_slice_in_dim(precond, sector * sector_width, sector_width, 2)
    initial = jnp.zeros((slab_count, comp_count, 2 * sector_width), jnp.float32)
    piece = lax.all_gather(residual, "sec", axis=2, tiled=True)
    span = piece.shape[2]
    table_rows = table
    flat = piece.reshape(-1, span)
    spectrum = jnp.dot(flat, table_rows, precision=lax.Precision.HIGHEST).reshape(initial.shape)
    scaled = scale_harmonics(own_inverse, spectrum).reshape(-1, 2 * sector_width)
    table_rows = table
    shares = lax.psum_scatter(
        lax.dot_general(
            table_rows, scaled, (((1,), (1,)), ((), ())), precision=lax.Precision.HIGHEST
        )
        / around_cells,
        "sec",
        scatter_dimension=0,
        tiled=True,
    )
    smoothed = shares.T.reshape(slab_count, comp_count, sector_width)
    prec = solid * smoothed
    image = solid * apply_operator(prec, stiffness)
    cell_total = slab_count * lax.axis_size("ax") * comp_count * around_cells
    inner_rz = lax.psum(jnp.sum(residual * prec), ("ax", "sec")) / cell_total
    inner_zq = lax.psum(jnp.sum(prec * image), ("ax", "sec")) / cell_total
    alpha = inner_rz / inner_zq
    residual_new = residual - alpha * image
    square_new = lax.psum(jnp.sum(residual_new * residual_new), ("ax", "sec")) / cell_total
    disp_new = disp + alpha * prec
    return (disp_new, residual_new, jnp.stack([inner_rz, inner_zq, square_new]))


def solution(mesh):
    in_specs = (
        P("ax", None, "sec"),
        P("ax", None, "sec"),
        P("ax", None, "sec"),
        P("ax", "sec"),
        P("ax"),
        P(),
        P(),
    )
    out_specs = (P("ax", None, "sec"), P("ax", None, "sec"), P())
    return jax.shard_map(shards, mesh=mesh, in_specs=in_specs, out_specs=out_specs, check_vma=False)
```

profile of v0, /device:TPU:1, one launch (start us, length us, event | category | flops | bytes accessed | tf_op | source)
XLA Modules:
  0.0 319.1 jit_solution(832956261714137729)
XLA Ops:
  7.3 2.3 fusion.30
  9.5 3.2 %collective-permute-start.2 = (f32[128,6,1]{2,0,1:T(8,128)}, f32[128,6,1]{2,0,1:T(8,128)S(1)}, u32[]{:S(2)}, u32[]{:S(2)}) collective-permute-start(f32[128,6,1]{2,0,1:T(8,128)} %get-tuple-element.16), channel_id=1, source_target_pairs={{1,0},{2,1},{3,2},{0,3},{5,4},{6,5},{7,6},{4,7},{9,8},{10,9},{11,1... | collective-permute-start | bytes 9224 | tf_op jit(solution)/shard_map/ppermute | solution.py:16
  12.8 1.1 collective-permute-start.3
  13.8 0.8 fusion.29
  14.7 1.3 collective-permute-start
  16.0 4.0 %collective-permute-start.1 = (f32[1,6,256]{2,0,1:T(1,128)S(1)}, f32[1,6,256]{2,0,1:T(1,128)S(1)}, u32[]{:S(2)}, u32[]{:S(2)}) collective-permute-start(f32[1,6,256]{2,0,1:T(1,128)S(1)} %get-tuple-element.15), channel_id=1, source_target_pairs={{0,4},{4,8},{8,12},{12,16},{16,20},{20,24},{24,28},{28,32},{32,36}... | collective-permute-start | bytes 18440 | tf_op jit(solution)/shard_map/ppermute | solution.py:15
  20.0 0.9 subtract_convert_fusion
  20.9 0.9 convolution_multiply_fusion.1
  22.0 1.1 collective-permute-done.3
  23.1 1.6 fusion.18
  25.0 4.1 %fusion.22 = (f32[1024,256]{1,0:T(8,128)S(1)}, f32[1024,256]{1,0:T(8,128)S(1)}) fusion(s32[256]{0:T(256)S(1)} %iota_add_fusion), kind=kLoop, calls=%fused_computation.47 | loop fusion | flops 3670016 | bytes 2098176 | tf_op jit(solution)/shard_map/cos | solution.py:38
  29.1 35.1 %all-gather.2.cloned.1.call-done = f32[128,6,1024]{2,0,1:T(8,128)} async-done(((f32[128,6,256]{2,0,1:T(8,128)}), f32[128,6,1024]{2,0,1:T(8,128)}) %all-gather.2.cloned.1.call-update) | async-done | bytes 3145744 | tf_op jit(solution)/shard_map/all_gather | solution.py:65
  64.1 7.0 %fusion = f32[128,6,512]{2,0,1:T(8,128)S(1)} fusion(f32[128,6,1024]{2,0,1:T(8,128)} %all-gather.2.cloned.1.call-done, f32[1024,256]{1,0:T(8,128)S(1)} %get-tuple-element.19, f32[1024,256]{1,0:T(8,128)S(1)} %get-tuple-element.18), kind=kOutput, calls=%fused_computation.2 | convolution fusion | flops 4832362496 | bytes 6815744 | tf_op jit(solution)/shard_map/dot_general | solution.py:69
  71.1 0.7 multiply_reduce_fusion
  71.8 2.3 copy.24
  74.1 2.6 reshape.48
  76.6 8.3 %convolution_multiply_fusion = f32[1024,768]{1,0:T(8,128)} fusion(f32[768,512]{1,0:T(8,128)} %reshape.48, f32[1024,256]{1,0:T(8,128)S(1)} %get-tuple-element.19, f32[1024,256]{1,0:T(8,128)S(1)} %get-tuple-element.18), kind=kOutput, calls=%fused_computation.4 | convolution fusion | flops 4833148928 | bytes 6815744 | tf_op jit(solution)/shard_map/dot_general | solution.py:73
  84.9 49.2 %reduce-scatter.2.cloned.1.call-done = f32[256,768]{1,0:T(8,128)} async-done(((f32[1024,768]{1,0:T(8,128)}), f32[256,768]{1,0:T(8,128)}) %reduce-scatter.2.cloned.1.call-update) | async-done | bytes 786448 | tf_op jit(solution)/shard_map/reduce_scatter | solution.py:72
  134.1 1.4 copy.25
  135.9 1.0 fusion.28
  137.0 2.6 reshape.50
  139.6 0.7 collective-permute-start.6
  140.3 2.6 collective-permute-start.7
  142.8 1.3 collective-permute-start.4
  144.1 4.0 %collective-permute-start.5 = (f32[1,6,256]{2,0,1:T(1,128)S(1)}, f32[1,6,256]{2,0,1:T(1,128)S(1)}, u32[]{:S(2)}, u32[]{:S(2)}) collective-permute-start(f32[1,6,256]{2,0,1:T(1,128)S(1)} %get-tuple-element.11), channel_id=1, source_target_pairs={{0,4},{4,8},{8,12},{12,16},{16,20},{20,24},{24,28},{28,32},{32,36}... | collective-permute-start | bytes 18440 | tf_op jit(solution)/shard_map/ppermute | solution.py:15
  148.1 1.2 copy_multiply_fusion
  149.4 3.3 %collective-permute-done.6 = f32[128,6,1]{2,0,1:T(8,128)S(1)} collective-permute-done((f32[128,6,1]{2,0,1:T(8,128)}, f32[128,6,1]{2,0,1:T(8,128)S(1)}, u32[]{:S(2)}, u32[]{:S(2)}) %collective-permute-start.6) | collective-permute-done | bytes 3104 | tf_op jit(solution)/shard_map/ppermute | solution.py:16
  152.8 2.2 multiply_reduce_fusion.2
  154.9 77.7 %all-reduce = (f32[]{:T(128)}, f32[]{:T(128)}) all-reduce(f32[]{:T(128)} %get-tuple-element.4, f32[]{:T(128)} %get-tuple-element.3), channel_id=1, replica_groups=mesh['ax'=64,'sec'=4] {'ax','sec'}, use_global_device_ids=true, to_apply=%region_3.4 | all-reduce | flops 2 | bytes 16 | tf_op jit(solution)/shard_map/psum | solution.py:85
  234.0 1.2 multiply_add_fusion
  235.2 1.6 multiply_reduce_fusion.1
  236.8 74.2 %psum.23 = f32[]{:T(128)} all-reduce(f32[]{:T(128)} %get-tuple-element.7), channel_id=1, replica_groups=mesh['ax'=64,'sec'=4] {'ax','sec'}, use_global_device_ids=true, to_apply=%region_7.8 | all-reduce | flops 1 | bytes 8 | tf_op jit(solution)/shard_map/psum | solution.py:89
  (40 shorter events, 1.5 us)
Async XLA Ops:
  7.2 17.8 %copy-start = (f32[6,6,1024]{2,1,0:T(8,128)S(1)}, f32[6,6,1024]{2,1,0:T(8,128)}, u32[]{:S(2)}) copy-start(f32[6,6,1024]{2,1,0:T(8,128)} %param.13) | copy-start | bytes 442372
  7.2 14.6 %copy-start.1 = (f32[128,6,256]{2,0,1:T(8,128)S(1)}, f32[128,6,256]{2,0,1:T(8,128)}, u32[]{:S(2)}) copy-start(f32[128,6,256]{2,0,1:T(8,128)} %param.8) | copy-start | bytes 2359300
  7.2 15.9 %copy-start.9 = (f32[128,6,256]{2,0,1:T(8,128)S(1)}, f32[128,6,256]{2,0,1:T(8,128)}, u32[]{:S(2)}) copy-start(f32[128,6,256]{2,0,1:T(8,128)} %param.7) | copy-start | bytes 2359300
  7.2 15.9 %copy-start.6 = (f32[128,6,256]{2,0,1:T(8,128)S(1)}, f32[128,6,256]{2,0,1:T(8,128)}, u32[]{:S(2)}) copy-start(f32[128,6,256]{2,0,1:T(8,128)} %param.9) | copy-start | bytes 2359300
  7.2 56.9 %all-gather.2.cloned.1.call-start = ((), (), s32[]{:S(2)}) async-start(), calls=%async_computation.1 | async-start | bytes 3932160 | tf_op jit(solution)/shard_map/all_gather | solution.py:65
  9.5 12.4 %collective-permute-start.2 = (f32[128,6,1]{2,0,1:T(8,128)}, f32[128,6,1]{2,0,1:T(8,128)S(1)}, u32[]{:S(2)}, u32[]{:S(2)}) collective-permute-start(f32[128,6,1]{2,0,1:T(8,128)} %get-tuple-element.16), channel_id=1, source_target_pairs={{1,0},{2,1},{3,2},{0,3},{5,4},{6,5},{7,6},{4,7},{9,8},{10,9},{11,1... | collective-permute-start | bytes 9224 | tf_op jit(solution)/shard_map/ppermute | solution.py:16
  12.8 10.3 %collective-permute-start.3 = (f32[128,6,1]{2,0,1:T(8,128)}, f32[128,6,1]{2,0,1:T(8,128)S(1)}, u32[]{:S(2)}, u32[]{:S(2)}) collective-permute-start(f32[128,6,1]{2,0,1:T(8,128)} %get-tuple-element.17), channel_id=1, source_target_pairs={{0,1},{1,2},{2,3},{3,0},{4,5},{5,6},{6,7},{7,4},{8,9},{9,10},{10,1... | collective-permute-start | bytes 9224 | tf_op jit(solution)/shard_map/ppermute | solution.py:15
  14.7 8.4 %collective-permute-start = (f32[1,6,256]{2,0,1:T(1,128)S(1)}, f32[1,6,256]{2,0,1:T(1,128)S(1)}, u32[]{:S(2)}, u32[]{:S(2)}) collective-permute-start(f32[1,6,256]{2,0,1:T(1,128)S(1)} %get-tuple-element.14), channel_id=1, source_target_pairs={{4,0},{8,4},{12,8},{16,12},{20,16},{24,20},{28,24},{32,28},{36,32}... | collective-permute-start | bytes 18440 | tf_op jit(solution)/shard_map/ppermute | solution.py:16
  16.0 7.1 %collective-permute-start.1 = (f32[1,6,256]{2,0,1:T(1,128)S(1)}, f32[1,6,256]{2,0,1:T(1,128)S(1)}, u32[]{:S(2)}, u32[]{:S(2)}) collective-permute-start(f32[1,6,256]{2,0,1:T(1,128)S(1)} %get-tuple-element.15), channel_id=1, source_target_pairs={{0,4},{4,8},{8,12},{12,16},{16,20},{20,24},{24,28},{28,32},{32,36}... | collective-permute-start | bytes 18440 | tf_op jit(solution)/shard_map/ppermute | solution.py:15
  24.7 109.5 %reduce-scatter.2.cloned.1.call-start = ((), (), s32[]{:S(2)}) async-start(), calls=%async_computation.2 | async-start | bytes 3932160 | tf_op jit(solution)/shard_map/reduce_scatter | solution.py:72
  135.5 1.4 copy-start.5
  135.9 1.1 copy-start.3
  137.0 15.8 %copy-start.2 = (f32[128,6,256]{2,0,1:T(8,128)S(1)}, f32[128,6,256]{2,0,1:T(8,128)}, u32[]{:S(2)}) copy-start(f32[128,6,256]{2,0,1:T(8,128)} %fusion.18) | copy-start | bytes 2359300
  139.6 13.2 %copy-start.4 = (f32[128,6,256]{2,0,1:T(8,128)S(1)}, f32[128,6,256]{2,0,1:T(8,128)}, u32[]{:S(2)}) copy-start(f32[128,6,256]{2,0,1:T(8,128)} %copy-done.3) | copy-start | bytes 2359300
  139.6 13.2 %copy-start.7 = (f32[128,6,256]{2,0,1:T(8,128)S(1)}, f32[128,6,256]{2,0,1:T(8,128)}, u32[]{:S(2)}) copy-start(f32[128,6,256]{2,0,1:T(8,128)} %param.9) | copy-start | bytes 2359300
  139.6 13.2 %collective-permute-start.6 = (f32[128,6,1]{2,0,1:T(8,128)}, f32[128,6,1]{2,0,1:T(8,128)S(1)}, u32[]{:S(2)}, u32[]{:S(2)}) collective-permute-start(f32[128,6,1]{2,0,1:T(8,128)} %get-tuple-element.12), channel_id=1, source_target_pairs={{1,0},{2,1},{3,2},{0,3},{5,4},{6,5},{7,6},{4,7},{9,8},{10,9},{11,1... | collective-permute-start | bytes 9224 | tf_op jit(solution)/shard_map/ppermute | solution.py:16
  140.3 12.5 %collective-permute-start.7 = (f32[128,6,1]{2,0,1:T(8,128)S(1)}, f32[128,6,1]{2,0,1:T(8,128)S(1)}, u32[]{:S(2)}, u32[]{:S(2)}) collective-permute-start(f32[128,6,1]{2,0,1:T(8,128)S(1)} %get-tuple-element.13), channel_id=1, source_target_pairs={{0,1},{1,2},{2,3},{3,0},{4,5},{5,6},{6,7},{7,4},{8,9},{9,10},{10,1... | collective-permute-start | bytes 9224 | tf_op jit(solution)/shard_map/ppermute | solution.py:15
  142.8 9.9 %collective-permute-start.4 = (f32[1,6,256]{2,0,1:T(1,128)S(1)}, f32[1,6,256]{2,0,1:T(1,128)S(1)}, u32[]{:S(2)}, u32[]{:S(2)}) collective-permute-start(f32[1,6,256]{2,0,1:T(1,128)S(1)} %get-tuple-element.10), channel_id=1, source_target_pairs={{4,0},{8,4},{12,8},{16,12},{20,16},{24,20},{28,24},{32,28},{36,32}... | collective-permute-start | bytes 18440 | tf_op jit(solution)/shard_map/ppermute | solution.py:16
  144.1 8.6 %collective-permute-start.5 = (f32[1,6,256]{2,0,1:T(1,128)S(1)}, f32[1,6,256]{2,0,1:T(1,128)S(1)}, u32[]{:S(2)}, u32[]{:S(2)}) collective-permute-start(f32[1,6,256]{2,0,1:T(1,128)S(1)} %get-tuple-element.11), channel_id=1, source_target_pairs={{0,4},{4,8},{8,12},{12,16},{16,20},{20,24},{24,28},{28,32},{32,36}... | collective-permute-start | bytes 18440 | tf_op jit(solution)/shard_map/ppermute | solution.py:15
  234.0 1.2 copy-start.8
Sparse Core Ops, SparseCore 0:
  24.8 39.2 all-gather.1
  85.0 49.0 reduce-scatter.1
where the time goes:
time: 320 us; the launch traced here: 319 us
  blocking collectives  152 us (48%)
  waiting for transfers between devices  88.8 us (28%)
  starting transfers between devices  18.4 us (6%)
  between operations  16.3 us (5%)
  matrix products  16.1 us (5%)
  other arithmetic  14.5 us (5%)
  local copies, waits for them, and re-layouts  13.1 us (4%)
    psum x1, blocking collectives, shards(): inner_rz = lax.psum(jnp.sum(residual * prec), ('ax', 'sec')) / cell_total  77.7 us
    psum x1, blocking collectives, shards(): lax.psum(jnp.sum(residual_new * residual_new), ('ax', 'sec')) / cell_total  74.2 us
    reduce_scatter x1, waiting for transfers between devices, shards(): lax.psum_scatter(lax.dot_general(table_rows, scaled, (((1,), (1,)), ((),...  49.2 us
    all_gather x1, waiting for transfers between devices, shards(): piece = lax.all_gather(residual, 'sec', axis=2, tiled=True)  35.1 us
    ppermute x4, starting transfers between devices, with_halo(): before = lax.ppermute(last, axis, up)  11.6 us
    dot_general x1, matrix products, shards(): lax.dot_general(table_rows, scaled, (((1,), (1,)), ((), ())), precision=l...  8.26 us
    dot_general x1, matrix products, shards(): jnp.dot(flat, table_rows, precision=lax.Precision.HIGHEST)  6.95 us
    ppermute x4, starting transfers between devices, with_halo(): after = lax.ppermute(first, axis, down)  6.5 us
  transfers between devices with their start and end apart: 10, of which 4 were waited for; matrix products, arithmetic and copies ran while one was open for 3% of the time, Pallas kernels for 0%

commit v1 on v0

--- a/solution.py
+++ b/solution.py
@@ -62,7 +62,10 @@
     table = harmonic_table(jnp.arange(around_cells), own_index, around_cells)
     own_inverse = lax.dynamic_slice_in_dim(precond, sector * sector_width, sector_width, 2)
     initial = jnp.zeros((slab_count, comp_count, 2 * sector_width), jnp.float32)
-    piece = lax.all_gather(residual, "sec", axis=2, tiled=True)
+    count = lax.axis_size("sec")
+    blocks = jnp.stack([residual for _ in range(count)])
+    blocks = lax.all_to_all(blocks, "sec", split_axis=0, concat_axis=0)
+    piece = jnp.concatenate(blocks, axis=2)
     span = piece.shape[2]
     table_rows = table
     flat = piece.reshape(-1, span)

time: 320 us -> 331 us (1.034)
  local copies, waits for them, and re-layouts: 13.1 us -> 20 us
  starting transfers between devices: 18.4 us -> 24.6 us
    all_gather x1 -> x0, waiting for transfers between devices: 35.1 us -> none  [shards(): piece = lax.all_gather(residual, 'sec', axis=2, tiled=True)]
    all_to_all x0 -> x1, waiting for transfers between devices: none -> 32.3 us  [shards(): blocks = lax.all_to_all(blocks, 'sec', split_axis=0, concat_axis=0)]
    all_to_all x0 -> x1, starting transfers between devices: none -> 6.45 us  [shards(): blocks = lax.all_to_all(blocks, 'sec', split_axis=0, concat_axis=0)]
    another operation x0 -> x2, local copies, waits for them, and re-layouts: none -> 4.47 us
where the time goes in v1:
time: 331 us
  blocking collectives  152 us (46%)
  waiting for transfers between devices  87.9 us (27%)
  starting transfers between devices  24.6 us (7%)
  local copies, waits for them, and re-layouts  20 us (6%)
  between operations  16.3 us (5%)
  other arithmetic  15.9 us (5%)
  matrix products  14.3 us (4%)
    psum x1, blocking collectives, shards(): inner_rz = lax.psum(jnp.sum(residual * prec), ('ax', 'sec')) / cell_total  77.5 us
    psum x1, blocking collectives, shards(): lax.psum(jnp.sum(residual_new * residual_new), ('ax', 'sec')) / cell_total  74.2 us
    reduce_scatter x1, waiting for transfers between devices, shards(): lax.psum_scatter(lax.dot_general(table_rows, scaled, (((1,), (1,)), ((),...  51.6 us
    all_to_all x1, waiting for transfers between devices, shards(): blocks = lax.all_to_all(blocks, 'sec', split_axis=0, concat_axis=0)  32.3 us
    ppermute x4, starting transfers between devices, with_halo(): before = lax.ppermute(last, axis, up)  11.6 us
    dot_general x1, matrix products, shards(): lax.dot_general(table_rows, scaled, (((1,), (1,)), ((), ())), precision=l...  8.18 us
  transfers between devices with their start and end apart: 10, of which 4 were waited for; matrix products, arithmetic and copies ran while one was open for 3% of the time, Pallas kernels for 0%

profile of v1, /device:TPU:1, one launch (start us, length us, event | category | flops | bytes accessed | tf_op | source)
XLA Modules:
  0.0 330.6 jit_solution(6690771843932140278)
XLA Ops:
  7.2 2.1 fusion.30
  9.2 3.2 collective-permute-start.2
  12.5 1.1 collective-permute-start.3
  14.4 1.3 collective-permute-start
  15.7 4.0 %collective-permute-start.1 = (f32[1,6,256]{2,0,1:T(1,128)S(1)}, f32[1,6,256]{2,0,1:T(1,128)S(1)}, u32[]{:S(2)}, u32[]{:S(2)}) collective-permute-start(f32[1,6,256]{2,0,1:T(1,128)S(1)} %get-tuple-element.18), channel_id=1, source_target_pairs={{0,4},{4,8},{8,12},{12,16},{16,20},{20,24},{24,28},{28,32},{32,36}... | collective-permute-start | bytes 18440 | tf_op jit(solution)/shard_map/ppermute | solution.py:15
  19.7 0.9 subtract_convert_fusion
  20.7 1.0 convolution_multiply_fusion.1
  23.0 1.7 fusion.18
  24.7 2.0 stack.19
  26.7 6.5 %all-to-all-start = ((f32[4,128,6,256]{3,1,2,0:T(8,128)}), f32[4,128,6,256]{3,1,2,0:T(8,128)}, u32[]{:S(2)}, u32[]{:S(2)}) async-start(f32[4,128,6,256]{3,1,2,0:T(8,128)} %stack.19), calls=%async_computation | async-start | bytes 6291456 | tf_op jit(solution)/shard_map/all_to_all | solution.py:67
  33.2 5.4 %fusion.22 = (f32[1024,256]{1,0:T(8,128)S(1)}, f32[1024,256]{1,0:T(8,128)}) fusion(s32[256]{0:T(256)S(1)} %iota_add_fusion), kind=kLoop, calls=%fused_computation.47 | loop fusion | flops 3670016 | bytes 2098176 | tf_op jit(solution)/shard_map/cos | solution.py:38
  38.6 32.3 %all-to-all-done = f32[4,128,6,256]{3,1,2,0:T(8,128)} async-done(((f32[4,128,6,256]{3,1,2,0:T(8,128)}), f32[4,128,6,256]{3,1,2,0:T(8,128)}, u32[]{:S(2)}, u32[]{:S(2)}) %all-to-all-start) | async-done | bytes 3145760 | tf_op jit(solution)/shard_map/all_to_all | solution.py:67
  70.9 2.4 copy.53
  73.3 5.1 %fusion = f32[128,6,512]{2,0,1:T(8,128)S(1)} fusion(f32[128,6,1024]{2,0,1:T(8,128)S(1)} %bitcast.20, f32[1024,256]{1,0:T(8,128)S(1)} %copy-done.2, f32[1024,256]{1,0:T(8,128)S(1)} %get-tuple-element.21), kind=kOutput, calls=%fused_computation.2 | convolution fusion | flops 4832362496 | bytes 6815744 | tf_op jit(solution)/shard_map/dot_general | solution.py:72
  79.1 2.3 copy.48
  81.4 2.6 reshape.56
  84.0 8.2 %convolution_multiply_fusion = f32[1024,768]{1,0:T(8,128)} fusion(f32[768,512]{1,0:T(8,128)} %reshape.56, f32[1024,256]{1,0:T(8,128)} %get-tuple-element.22, f32[1024,256]{1,0:T(8,128)S(1)} %get-tuple-element.21), kind=kOutput, calls=%fused_computation.4 | convolution fusion | flops 4833148928 | bytes 6815744 | tf_op jit(solution)/shard_map/dot_general | solution.py:76
  92.2 51.6 %reduce-scatter.2.cloned.1.call-done = f32[256,768]{1,0:T(8,128)} async-done(((f32[1024,768]{1,0:T(8,128)}), f32[256,768]{1,0:T(8,128)}) %reduce-scatter.2.cloned.1.call-update) | async-done | bytes 786448 | tf_op jit(solution)/shard_map/reduce_scatter | solution.py:75
  143.8 2.3 copy.49
  146.1 1.2 reshape.57
  147.6 1.0 fusion.28
  148.6 2.5 reshape.58
  151.8 2.6 collective-permute-start.7
  154.4 1.3 collective-permute-start.4
  155.6 4.0 %collective-permute-start.5 = (f32[1,6,256]{2,0,1:T(1,128)S(1)}, f32[1,6,256]{2,0,1:T(1,128)S(1)}, u32[]{:S(2)}, u32[]{:S(2)}) collective-permute-start(f32[1,6,256]{2,0,1:T(1,128)S(1)} %get-tuple-element.14), channel_id=1, source_target_pairs={{0,4},{4,8},{8,12},{12,16},{16,20},{20,24},{24,28},{28,32},{32,36}... | collective-permute-start | bytes 18440 | tf_op jit(solution)/shard_map/ppermute | solution.py:15
  159.6 1.2 copy_multiply_fusion
  160.9 3.5 %collective-permute-done.6 = f32[128,6,1]{2,0,1:T(8,128)S(1)} collective-permute-done((f32[128,6,1]{2,0,1:T(8,128)}, f32[128,6,1]{2,0,1:T(8,128)S(1)}, u32[]{:S(2)}, u32[]{:S(2)}) %collective-permute-start.6) | collective-permute-done | bytes 3104 | tf_op jit(solution)/shard_map/ppermute | solution.py:16
  164.5 2.2 multiply_reduce_fusion.2
  166.6 77.5 %all-reduce = (f32[]{:T(128)}, f32[]{:T(128)}) all-reduce(f32[]{:T(128)} %get-tuple-element.7, f32[]{:T(128)} %get-tuple-element.6), channel_id=1, replica_groups=mesh['ax'=64,'sec'=4] {'ax','sec'}, use_global_device_ids=true, to_apply=%region_3.4 | all-reduce | flops 2 | bytes 16 | tf_op jit(solution)/shard_map/psum | solution.py:88
  245.5 1.2 multiply_add_fusion
  246.7 1.6 multiply_reduce_fusion.1
  248.3 74.2 %psum.23 = f32[]{:T(128)} all-reduce(f32[]{:T(128)} %get-tuple-element.10), channel_id=1, replica_groups=mesh['ax'=64,'sec'=4] {'ax','sec'}, use_global_device_ids=true, to_apply=%region_7.8 | all-reduce | flops 1 | bytes 8 | tf_op jit(solution)/shard_map/psum | solution.py:92
  (41 shorter events, 4.6 us)
Async XLA Ops:
  7.2 26.0 %copy-start = (f32[6,6,1024]{2,1,0:T(8,128)S(1)}, f32[6,6,1024]{2,1,0:T(8,128)}, u32[]{:S(2)}) copy-start(f32[6,6,1024]{2,1,0:T(8,128)} %param.13) | copy-start | bytes 442372
  7.2 14.5 %copy-start.1 = (f32[128,6,256]{2,0,1:T(8,128)S(1)}, f32[128,6,256]{2,0,1:T(8,128)}, u32[]{:S(2)}) copy-start(f32[128,6,256]{2,0,1:T(8,128)} %param.8) | copy-start | bytes 2359300
  9.2 12.6 %collective-permute-start.2 = (f32[128,6,1]{2,0,1:T(8,128)}, f32[128,6,1]{2,0,1:T(8,128)S(1)}, u32[]{:S(2)}, u32[]{:S(2)}) collective-permute-start(f32[128,6,1]{2,0,1:T(8,128)} %get-tuple-element.19), channel_id=1, source_target_pairs={{1,0},{2,1},{3,2},{0,3},{5,4},{6,5},{7,6},{4,7},{9,8},{10,9},{11,1... | collective-permute-start | bytes 9224 | tf_op jit(solution)/shard_map/ppermute | solution.py:16
  12.5 9.8 %collective-permute-start.3 = (f32[128,6,1]{2,0,1:T(8,128)S(1)}, f32[128,6,1]{2,0,1:T(8,128)S(1)}, u32[]{:S(2)}, u32[]{:S(2)}) collective-permute-start(f32[128,6,1]{2,0,1:T(8,128)S(1)} %get-tuple-element.20), channel_id=1, source_target_pairs={{0,1},{1,2},{2,3},{3,0},{4,5},{5,6},{6,7},{7,4},{8,9},{9,10},{10,1... | collective-permute-start | bytes 9224 | tf_op jit(solution)/shard_map/ppermute | solution.py:15
  14.4 7.9 %collective-permute-start = (f32[1,6,256]{2,0,1:T(1,128)S(1)}, f32[1,6,256]{2,0,1:T(1,128)S(1)}, u32[]{:S(2)}, u32[]{:S(2)}) collective-permute-start(f32[1,6,256]{2,0,1:T(1,128)S(1)} %get-tuple-element.17), channel_id=1, source_target_pairs={{4,0},{8,4},{12,8},{16,12},{20,16},{24,20},{28,24},{32,28},{36,32}... | collective-permute-start | bytes 18440 | tf_op jit(solution)/shard_map/ppermute | solution.py:16
  15.7 7.3 %collective-permute-start.1 = (f32[1,6,256]{2,0,1:T(1,128)S(1)}, f32[1,6,256]{2,0,1:T(1,128)S(1)}, u32[]{:S(2)}, u32[]{:S(2)}) collective-permute-start(f32[1,6,256]{2,0,1:T(1,128)S(1)} %get-tuple-element.18), channel_id=1, source_target_pairs={{0,4},{4,8},{8,12},{12,16},{16,20},{20,24},{24,28},{28,32},{32,36}... | collective-permute-start | bytes 18440 | tf_op jit(solution)/shard_map/ppermute | solution.py:15
  20.6 2.4 copy-start.5
  20.7 2.4 copy-start.8
  22.3 0.7 copy-start.9
  26.7 44.1 %all-to-all-start = ((f32[4,128,6,256]{3,1,2,0:T(8,128)}), f32[4,128,6,256]{3,1,2,0:T(8,128)}, u32[]{:S(2)}, u32[]{:S(2)}) async-start(f32[4,128,6,256]{3,1,2,0:T(8,128)} %stack.19), calls=%async_computation | async-start | bytes 6291456 | tf_op jit(solution)/shard_map/all_to_all | solution.py:67
  33.2 110.6 %reduce-scatter.2.cloned.1.call-start = ((), (), s32[]{:S(2)}) async-start(), calls=%async_computation.2 | async-start | bytes 3932160 | tf_op jit(solution)/shard_map/reduce_scatter | solution.py:75
  70.9 2.5 copy-start.2
  147.6 1.0 copy-start.3
  151.1 13.4 %copy-start.4 = (f32[128,6,256]{2,0,1:T(8,128)S(1)}, f32[128,6,256]{2,0,1:T(8,128)}, u32[]{:S(2)}) copy-start(f32[128,6,256]{2,0,1:T(8,128)} %copy-done.3) | copy-start | bytes 2359300
  151.1 13.4 %copy-start.6 = (f32[128,6,256]{2,0,1:T(8,128)S(1)}, f32[128,6,256]{2,0,1:T(8,128)}, u32[]{:S(2)}) copy-start(f32[128,6,256]{2,0,1:T(8,128)} %param.9) | copy-start | bytes 2359300
  151.1 13.3 %collective-permute-start.6 = (f32[128,6,1]{2,0,1:T(8,128)}, f32[128,6,1]{2,0,1:T(8,128)S(1)}, u32[]{:S(2)}, u32[]{:S(2)}) collective-permute-start(f32[128,6,1]{2,0,1:T(8,128)} %get-tuple-element.15), channel_id=1, source_target_pairs={{1,0},{2,1},{3,2},{0,3},{5,4},{6,5},{7,6},{4,7},{9,8},{10,9},{11,1... | collective-permute-start | bytes 9224 | tf_op jit(solution)/shard_map/ppermute | solution.py:16
  151.8 12.7 %collective-permute-start.7 = (f32[128,6,1]{2,0,1:T(8,128)S(1)}, f32[128,6,1]{2,0,1:T(8,128)S(1)}, u32[]{:S(2)}, u32[]{:S(2)}) collective-permute-start(f32[128,6,1]{2,0,1:T(8,128)S(1)} %get-tuple-element.16), channel_id=1, source_target_pairs={{0,1},{1,2},{2,3},{3,0},{4,5},{5,6},{6,7},{7,4},{8,9},{9,10},{10,1... | collective-permute-start | bytes 9224 | tf_op jit(solution)/shard_map/ppermute | solution.py:15
  154.4 10.1 %collective-permute-start.4 = (f32[1,6,256]{2,0,1:T(1,128)S(1)}, f32[1,6,256]{2,0,1:T(1,128)S(1)}, u32[]{:S(2)}, u32[]{:S(2)}) collective-permute-start(f32[1,6,256]{2,0,1:T(1,128)S(1)} %get-tuple-element.13), channel_id=1, source_target_pairs={{4,0},{8,4},{12,8},{16,12},{20,16},{24,20},{28,24},{32,28},{36,32}... | collective-permute-start | bytes 18440 | tf_op jit(solution)/shard_map/ppermute | solution.py:16
  155.6 8.8 %collective-permute-start.5 = (f32[1,6,256]{2,0,1:T(1,128)S(1)}, f32[1,6,256]{2,0,1:T(1,128)S(1)}, u32[]{:S(2)}, u32[]{:S(2)}) collective-permute-start(f32[1,6,256]{2,0,1:T(1,128)S(1)} %get-tuple-element.14), channel_id=1, source_target_pairs={{0,4},{4,8},{8,12},{12,16},{16,20},{20,24},{24,28},{28,32},{32,36}... | collective-permute-start | bytes 18440 | tf_op jit(solution)/shard_map/ppermute | solution.py:15
  245.5 1.2 copy-start.7
Sparse Core Ops, SparseCore 0:
  92.3 51.4 reduce-scatter.1
